TPU v7x, 32 devices: a whole 2x2x4 slice. The times are simulated.
32 devices in a mesh: ctx: 8 (over z, x), head: 4 (over y, core).
Axes of the slice: x: 2, y: 2, z: 4, core: 2. Of those that a mesh axis runs over, the one named last changes fastest.
Arguments:
- query: bfloat16 [8, 2, 128, 8192], P('ctx', None, 'head'), may hold values from -200 to 200
- keyval: bfloat16 [8, 2, 2, 128, 1024], P('ctx', None, None, 'head'), may hold values from -6 to 6
- doc_blocks: int32 [4], replicated, may hold values from 1 to 12, 16 in all
Outputs:
- attended: bfloat16 [8, 2, 128, 8192], P('ctx', None, 'head')
Inputs may be any that keep to these rules, and one draw needn't show every extreme that they name: `doc_blocks`: documents fill the sequence in order; the longest has exactly 12 blocks.
All inputs are finite; a program needn't handle non-finite values.
Results may differ from a plain program's by a relative error of at most 0.0038.
Values may be sent and summed in bfloat16 or wider, within the bound.
A program may use at most 64 MiB of HBM per device.

v0:
```python
import jax
import jax.numpy as jnp
from jax import lax
from jax.sharding import PartitionSpec as P

QUERY_HEADS = 64
KEY_VALUE_HEADS = 8
HEAD_WIDTH = 128
BLK = 128


def doc_index(positions, doc_ends):
    return jnp.sum((positions[:, None] >= doc_ends[None, :]).astype(jnp.int32), axis=1)


def local(query, keyval, doc_blocks):
    ctx_count = lax.axis_size("ctx")
    ctx_index = lax.axis_index("ctx")
    span_len = query.shape[2] * lax.axis_size("head")
    width_kv = keyval.shape[4]
    stacked = keyval.reshape(1, 4, keyval.shape[3], width_kv)
    query_heads, kv_heads = (
        lax.all_to_all(query, "head", split_axis=3, concat_axis=2, tiled=True),
        lax.all_to_all(stacked, "head", split_axis=3, concat_axis=2, tiled=True),
    )
    kv_local = kv_heads.shape[3] // HEAD_WIDTH
    heads_per_group = QUERY_HEADS // KEY_VALUE_HEADS
    kv_mine = kv_heads.reshape(1, 2, 2, span_len, kv_local * HEAD_WIDTH)
    row_count = 2 * span_len
    query_rows = query_heads.reshape(row_count, kv_local, heads_per_group, HEAD_WIDTH)
    offsets = jnp.arange(span_len, dtype=jnp.int32)
    query_pos = jnp.concatenate(
        [ctx_index * span_len + offsets, (2 * ctx_count - 1 - ctx_index) * span_len + offsets]
    )
    doc_ends = jnp.cumsum(doc_blocks) * BLK
    query_doc = doc_index(query_pos, doc_ends)
    scale_factor = HEAD_WIDTH ** (-0.5)
    initial = (
        jnp.full((kv_local, heads_per_group, row_count), -1e30, jnp.float32),
        jnp.zeros((kv_local, heads_per_group, row_count), jnp.float32),
        jnp.zeros((row_count, kv_local, heads_per_group, HEAD_WIDTH), jnp.float32),
    )
    gathered = lax.all_gather(kv_mine, "ctx", axis=0, tiled=True)
    running = initial
    count = gathered.shape[0]
    group_size = 4
    group_count = count // group_size
    grouped = gathered.reshape(group_count, group_size, 2, 2, span_len, kv_local * HEAD_WIDTH)
    firsts = jnp.arange(group_count, dtype=jnp.int32) * group_size

    def advance(state, payload):
        block_kv, lead_span = payload
        span_ids = lead_span + jnp.arange(group_size, dtype=jnp.int32)
        lower_pos = span_ids[:, None] * span_len + offsets[None, :]
        upper_pos = (2 * ctx_count - 1 - span_ids)[:, None] * span_len + offsets[None, :]
        key_pos = jnp.stack([lower_pos, upper_pos], axis=1).reshape(-1)
        key_row_block = block_kv[:, 0].reshape(-1, kv_local, HEAD_WIDTH)
        value_rows = block_kv[:, 1].reshape(-1, kv_local, HEAD_WIDTH)
        visible = (query_doc[:, None] == doc_index(key_pos, doc_ends)[None, :]) & (
            key_pos[None, :] <= query_pos[:, None]
        )
        row_max, totals, acc_sum = state
        scores = (
            jnp.einsum(
                "rgjd,kgd->gjrk", query_rows, key_row_block, preferred_element_type=jnp.float32
            )
            * scale_factor
        )
        scores = jnp.where(visible[None, None], scores, -1e30)
        new_max = jnp.maximum(row_max, jnp.max(scores, axis=-1))
        probs = jnp.where(visible[None, None], jnp.exp(scores - new_max[..., None]), 0.0)
        rescale = jnp.exp(row_max - new_max)
        totals = totals * rescale + jnp.sum(probs, axis=-1)
        added = jnp.einsum(
            "gjrk,kgd->rgjd",
            probs.astype(jnp.bfloat16),
            value_rows,
            preferred_element_type=jnp.float32,
        )
        acc_sum = acc_sum * jnp.moveaxis(rescale, 2, 0)[..., None] + added
        state = (new_max, totals, acc_sum)
        return (state, None)

    running, _ = lax.scan(advance, running, (grouped, firsts))
    row_max, totals, acc_sum = running
    result = (acc_sum / jnp.moveaxis(totals, 2, 0)[..., None]).astype(jnp.bfloat16)
    result = result.reshape(1, 2, span_len, kv_local * heads_per_group * HEAD_WIDTH)
    return lax.all_to_all(result, "head", split_axis=2, concat_axis=3, tiled=True)


def solution(mesh):
    placed = (P("ctx", None, "head", None), P("ctx", None, None, "head", None), P())
    return jax.shard_map(
        local, mesh=mesh, in_specs=placed, out_specs=P("ctx", None, "head", None), check_vma=False
    )
```

profile of v0, /device:TPU:0, one launch (start us, length us, event | category | flops | bytes accessed | tf_op | source)
XLA Modules:
  0.0 154.3 jit_solution(14284918072613798459)
XLA Ops:
  6.5 0.0 copy-start.1
  6.5 0.0 all-gather.2.cloned.1.call-start
  6.5 2.2 %copy.50 = bf16[1,2,2,32,1024]{3,2,1,4,0:T(2,128)(2,1)S(1)} copy(bf16[1,2,2,32,1024]{4,3,2,1,0:T(8,128)(2,1)} %param.6) | data formatting | bytes 524288 | tf_op args[1]
  8.8 1.0 reshape.201
  9.7 10.1 %all_to_all.48 = bf16[4,2,16384]{2,1,0:T(2,128)(2,1)S(1)} all-to-all(bf16[4,2,16384]{2,1,0:T(2,128)(2,1)S(1)} %reshape.201), channel_id=1, replica_groups=mesh['ctx'=8,'head'=4] {'head'}, dimensions={0} | all-to-all | bytes 524288 | tf_op jit(solution)/shard_map/all_to_all | solution.py:24
  19.8 0.5 reshape.202
  20.3 0.7 copy.64
  21.0 0.7 copy.52
  21.7 0.0 all-gather.2.cloned.1.call-update
  21.8 9.2 %copy.53 = bf16[1,2,32,8192]{2,1,0,3:T(2,128)(2,1)} copy(bf16[1,2,32,8192]{3,2,1,0:T(8,128)(2,1)} %param.5) | data formatting | bytes 2097152 | tf_op args[0]
  30.9 6.4 %reshape.203 = bf16[4,2,65536]{2,1,0:T(2,128)(2,1)} reshape(bf16[8192,1,2,32]{3,2,1,0:T(2,128)(2,1)} %bitcast.85) | data formatting | bytes 2097152
  37.3 3.5 %all-to-all-start.1 = ((bf16[4,2,65536]{2,1,0:T(2,128)(2,1)}), bf16[4,2,65536]{2,1,0:T(2,128)(2,1)S(1)}, u32[]{:S(2)}, u32[]{:S(2)}) async-start(bf16[4,2,65536]{2,1,0:T(2,128)(2,1)} %reshape.203), calls=%async_computation.1 | async-start | bytes 2097152 | tf_op jit(solution)/shard_map/all_to_all | solution.py:23
  40.9 0.0 copy-done.1
  40.9 0.2 reduce-window.7
  41.1 0.1 convert_reduce_fusion.1
  41.2 14.1 %all-to-all-done.1 = bf16[4,2,65536]{2,1,0:T(2,128)(2,1)S(1)} async-done(((bf16[4,2,65536]{2,1,0:T(2,128)(2,1)}), bf16[4,2,65536]{2,1,0:T(2,128)(2,1)S(1)}, u32[]{:S(2)}, u32[]{:S(2)}) %all-to-all-start.1) | async-done | bytes 1048608 | tf_op jit(solution)/shard_map/all_to_all | solution.py:23
  55.3 3.5 %reshape.204 = bf16[8192,1,2,32]{3,2,1,0:T(2,128)(2,1)} reshape(bf16[4,2,65536]{2,1,0:T(2,128)(2,1)S(1)} %all-to-all-done.1) | data formatting | bytes 2097152
  58.8 9.0 %copy.54 = bf16[1,2,32,4,2048]{4,2,3,1,0:T(8,128)(2,1)S(1)} copy(bf16[1,2,32,4,2048]{2,1,4,3,0:T(2,128)(2,1)} %bitcast.84) | data formatting | bytes 2097152 | tf_op jit(solution)/shard_map/all_to_all | solution.py:23
  67.7 0.2 copy.74
  68.0 0.3 copy.56
  68.3 3.1 %all-gather.2.cloned.1.call-done = bf16[8,2,2,128,256]{4,3,2,1,0:T(8,128)(2,1)} async-done(((bf16[1,2,2,128,256]{4,3,2,1,0:T(8,128)(2,1)}), bf16[8,2,2,128,256]{4,3,2,1,0:T(8,128)(2,1)}) %all-gather.2.cloned.1.call-update) | async-done | bytes 2097168 | tf_op jit(solution)/shard_map/all_gather | solution.py:43
  71.3 52.6 %while.16 = (s32[]{:T(128)}, f32[2,8,256]{2,1,0:T(8,128)S(1)}, f32[2,8,256]{2,1,0:T(8,128)S(1)}, f32[256,2,8,128]{0,3,2,1:T(8,128)}, s32[256]{0:T(256)S(1)}, /*i...) while((s32[]{:T(128)}, f32[2,8,256]{2,1,0:T(8,128)S(1)}, ...), condition=%wide.region_6.7_spmd.clone.clone, body=%wide.region_2.6_spmd.clone.clone.sunk | while | flops 2204406784 | bytes 131365624 | solution.py:84
  71.3 0.6 dynamic_slice.17
  71.9 0.6 subtract_multiply_fusion.2
  72.6 0.1 iota_add_fusion.7
  72.7 0.1 iota_add_fusion.8
  72.7 0.1 convert_reduce_fusion.3
  72.8 0.3 compare_and_fusion.2
  73.2 1.3 copy_bitcast_fusion.2
  74.5 0.1 fusion.32
  74.6 0.1 squeeze.23
  74.7 7.2 %fusion.33 = (f32[2,8,256]{2,1,0:T(8,128)S(1)}, f32[2,1024,256,8]{2,1,3,0:T(8,128)}) fusion(pred[256,1024]{0,1:T(8,128)(4,1)S(1)} %compare_and_fusion.2, bf16[256,2,8,128]{3,0,2,1:T(8,128)(2,1)S(1)} %get-tuple-element.319, bf16[1024,2,128,1]{2,1,0,3:T(2,128)(2,1)S(1)} %bitcast.83), kind=kOutput, calls=%fused_computation.3.clone.1 | convolution fusion | flops 1086320640 | bytes 18628608 | tf_op jit(solution)/shard_map/while/body/eval_jaxpr/rgjd,kgd->gjrk/dot_general | solution.py:64
  81.9 0.1 reshape.206
  82.0 0.0 copy-start
  82.0 9.7 %bitcast_add_fusion.2 = f32[256,2,8,128]{0,3,2,1:T(8,128)} fusion(f32[256,2,8,128]{0,3,2,1:T(8,128)} %get-tuple-element.301, f32[2,1024,256,8]{2,1,3,0:T(8,128)} %get-tuple-element.283, f32[2,8,256]{2,1,0:T(8,128)S(1)} %get-tuple-element.311, pred[256,1024]{0,1:T(8,128)(4,1)S(1)} %compare_and_fusion.2, f32[256,2,8]{0,2,1:T(8,128)S(1)} %get-tuple-element.284, ...), kind=kOutput, calls=%fused_computation.8.clone.1 | convolution fusion | flops 1096286208 | bytes 21790720 | tf_op jit(solution)/shard_map/while/body/eval_jaxpr/gjrk,kgd->rgjd/dot_general | solution.py:74
  91.7 1.6 %copy-done = f32[2,1024,256,8]{2,1,3,0:T(8,128)S(1)} copy-done((f32[2,1024,256,8]{2,1,3,0:T(8,128)S(1)}, f32[2,1024,256,8]{2,1,3,0:T(8,128)}, u32[]{:S(2)}) %copy-start) | copy-done | bytes 16777240 | tf_op jit(solution)/shard_map/while
  93.3 4.0 %fusion.35 = f32[2,8,256]{2,1,0:T(8,128)S(1)} fusion(f32[2,1024,256,8]{2,1,3,0:T(8,128)S(1)} %copy-done, f32[2,8,256]{2,1,0:T(8,128)S(1)} %get-tuple-element.311, pred[256,1024]{0,1:T(8,128)(4,1)S(1)} %compare_and_fusion.2), kind=kLoop, calls=%fused_computation.5.clone.1 | loop fusion | flops 20967424 | bytes 17072128 | tf_op jit(solution)/shard_map/while/body/eval_jaxpr/reduce_sum | solution.py:73
  97.4 0.6 dynamic_slice.17
  97.9 0.6 subtract_multiply_fusion.2
  98.6 0.1 iota_add_fusion.7
  98.7 0.1 iota_add_fusion.8
  98.8 0.1 convert_reduce_fusion.3
  98.8 0.3 compare_and_fusion.2
  99.2 1.3 copy_bitcast_fusion.2
  100.5 0.1 fusion.32
  100.6 0.1 squeeze.23
  100.7 7.2 %fusion.33 = (f32[2,8,256]{2,1,0:T(8,128)S(1)}, f32[2,1024,256,8]{2,1,3,0:T(8,128)}) fusion(pred[256,1024]{0,1:T(8,128)(4,1)S(1)} %compare_and_fusion.2, bf16[256,2,8,128]{3,0,2,1:T(8,128)(2,1)S(1)} %get-tuple-element.319, bf16[1024,2,128,1]{2,1,0,3:T(2,128)(2,1)S(1)} %bitcast.83), kind=kOutput, calls=%fused_computation.3.clone.1 | convolution fusion | flops 1086320640 | bytes 18628608 | tf_op jit(solution)/shard_map/while/body/eval_jaxpr/rgjd,kgd->gjrk/dot_general | solution.py:64
  107.9 0.1 reshape.206
  108.0 0.0 copy-start
  108.1 10.3 %bitcast_add_fusion.2 = f32[256,2,8,128]{0,3,2,1:T(8,128)} fusion(f32[256,2,8,128]{0,3,2,1:T(8,128)} %get-tuple-element.301, f32[2,1024,256,8]{2,1,3,0:T(8,128)} %get-tuple-element.283, f32[2,8,256]{2,1,0:T(8,128)S(1)} %get-tuple-element.311, pred[256,1024]{0,1:T(8,128)(4,1)S(1)} %compare_and_fusion.2, f32[256,2,8]{0,2,1:T(8,128)S(1)} %get-tuple-element.284, ...), kind=kOutput, calls=%fused_computation.8.clone.1 | convolution fusion | flops 1096286208 | bytes 21790720 | tf_op jit(solution)/shard_map/while/body/eval_jaxpr/gjrk,kgd->rgjd/dot_general | solution.py:74
  118.3 1.6 %copy-done = f32[2,1024,256,8]{2,1,3,0:T(8,128)S(1)} copy-done((f32[2,1024,256,8]{2,1,3,0:T(8,128)S(1)}, f32[2,1024,256,8]{2,1,3,0:T(8,128)}, u32[]{:S(2)}) %copy-start) | copy-done | bytes 16777240 | tf_op jit(solution)/shard_map/while
  119.9 4.0 %fusion.35 = f32[2,8,256]{2,1,0:T(8,128)S(1)} fusion(f32[2,1024,256,8]{2,1,3,0:T(8,128)S(1)} %copy-done, f32[2,8,256]{2,1,0:T(8,128)S(1)} %get-tuple-element.311, pred[256,1024]{0,1:T(8,128)(4,1)S(1)} %compare_and_fusion.2), kind=kLoop, calls=%fused_computation.5.clone.1 | loop fusion | flops 20967424 | bytes 17072128 | tf_op jit(solution)/shard_map/while/body/eval_jaxpr/reduce_sum | solution.py:73
  124.0 1.8 %divide_convert_fusion = bf16[256,2,8,128]{0,3,2,1:T(8,128)(2,1)S(1)} fusion(f32[256,2,8,128]{0,3,2,1:T(8,128)} %get-tuple-element.66, f32[256,2,8]{0,2,1:T(8,128)S(1)} %bitcast.97), kind=kLoop, calls=%fused_computation.31 | loop fusion | flops 1048576 | bytes 3162112 | tf_op jit(solution)/shard_map/convert_element_type | solution.py:86
  125.8 0.3 reshape.199
  126.1 3.1 %copy.58 = bf16[1,2,128,2048]{3,1,0,2:T(2,128)(2,1)S(1)} copy(bf16[1,2,128,2048]{2,1,3,0:T(2,128)(2,1)S(1)} %reshape.199) | data formatting | bytes 2097152 | tf_op jit(solution)/shard_map/reshape | solution.py:87
  129.1 17.0 %all_to_all.49 = bf16[1,2,128,2048]{3,1,0,2:T(2,128)(2,1)S(1)} all-to-all(bf16[1,2,128,2048]{3,1,0,2:T(2,128)(2,1)S(1)} %copy.58), channel_id=1, replica_groups=mesh['ctx'=8,'head'=4] {'head'}, dimensions={2} | all-to-all | bytes 2097152 | tf_op jit(solution)/shard_map/all_to_all | solution.py:88
  146.1 0.3 copy.59
  146.5 1.0 copy.73
  (15 shorter events, 0.1 us)
Async XLA Ops:
  6.5 34.4 %copy-start.1 = (s32[4]{0:T(128)S(1)}, s32[4]{0:T(128)}, u32[]{:S(2)}) copy-start(s32[4]{0:T(128)} %param.7) | copy-start | bytes 52
  6.5 64.8 %all-gather.2.cloned.1.call-start = ((), (), s32[]{:S(2)}) async-start(), calls=%async_computation.3 | async-start | bytes 2359296 | tf_op jit(solution)/shard_map/all_gather | solution.py:43
  37.3 17.9 %all-to-all-start.1 = ((bf16[4,2,65536]{2,1,0:T(2,128)(2,1)}), bf16[4,2,65536]{2,1,0:T(2,128)(2,1)S(1)}, u32[]{:S(2)}, u32[]{:S(2)}) async-start(bf16[4,2,65536]{2,1,0:T(2,128)(2,1)} %reshape.203), calls=%async_computation.1 | async-start | bytes 2097152 | tf_op jit(solution)/shard_map/all_to_all | solution.py:23
  82.0 11.3 %copy-start = (f32[2,1024,256,8]{2,1,3,0:T(8,128)S(1)}, f32[2,1024,256,8]{2,1,3,0:T(8,128)}, u32[]{:S(2)}) copy-start(f32[2,1024,256,8]{2,1,3,0:T(8,128)} %get-tuple-element.283) | copy-start | bytes 50331652 | tf_op jit(solution)/shard_map/while
  108.0 11.9 %copy-start = (f32[2,1024,256,8]{2,1,3,0:T(8,128)S(1)}, f32[2,1024,256,8]{2,1,3,0:T(8,128)}, u32[]{:S(2)}) copy-start(f32[2,1024,256,8]{2,1,3,0:T(8,128)} %get-tuple-element.283) | copy-start | bytes 50331652 | tf_op jit(solution)/shard_map/while
Sparse Core Ops, SparseCore 0:
  21.9 49.4 all-gather.1
where the time goes:
time: 156 us; the launch traced here: 154 us
  local copies, waits for them, and re-layouts  46 us (29%)
  matrix products  34.3 us (22%)
  blocking collectives  27 us (17%)
  waiting for transfers between devices  17.2 us (11%)
  between operations  13.5 us (9%)
  other arithmetic  12.5 us (8%)
  starting transfers between devices  3.52 us (2%)
    unnamed x10, local copies, waits for them, and re-layouts  23.3 us
    dot_general x2, matrix products, advance(): jnp.einsum('gjrk,kgd->rgjd', probs.astype(jnp.bfloat16), value_rows, pref...  20 us
    all_to_all x1, blocking collectives, local(): lax.all_to_all(result, 'head', split_axis=2, concat_axis=3, tiled=True)  17 us
    dot_general x2, matrix products, advance(): jnp.einsum('rgjd,kgd->gjrk', query_rows, key_row_block, preferred_element...  14.3 us
    all_to_all x1, waiting for transfers between devices, local(): lax.all_to_all(query, 'head', split_axis=3, concat_axis=2, tiled=True)  14.1 us
    all_to_all x1, blocking collectives, local(): lax.all_to_all(stacked, 'head', split_axis=3, concat_axis=2, tiled=True)  10.1 us
    all_to_all x1, local copies, waits for them, and re-layouts, local(): lax.all_to_all(query, 'head', split_axis=3, concat_axis=2, tiled=True)  8.96 us
    reduce_sum x2, other arithmetic, advance(): totals = totals * rescale + jnp.sum(probs, axis=-1)  7.97 us
  transfers between devices with their start and end apart: 2, of which 2 were waited for; matrix products, arithmetic and copies ran while one was open for 19% of the time, Pallas kernels for 0%

commit v1 on v0

--- a/solution.py
+++ b/solution.py
@@ -7,6 +7,22 @@
 KEY_VALUE_HEADS = 8
 HEAD_WIDTH = 128
 BLK = 128
+
+
+def exchange_in_pairs(x, axis, split, join):
+    ways, here = (lax.axis_size(axis), lax.axis_index(axis))
+    width = x.shape[split] // ways
+    dims = list(x.shape)
+    dims[split] = width
+    height = dims[join]
+    dims[join] = height * ways
+    full = jnp.zeros(dims, x.dtype)
+    for mask in range(ways):
+        part = lax.dynamic_slice_in_dim(x, (here ^ mask) * width, width, axis=split)
+        if mask:
+            part = lax.ppermute(part, axis, [(d, d ^ mask) for d in range(ways)])
+        full = lax.dynamic_update_slice_in_dim(full, part, (here ^ mask) * height, axis=join)
+    return full
 
 
 def doc_index(positions, doc_ends):
@@ -21,7 +37,7 @@
     stacked = keyval.reshape(1, 4, keyval.shape[3], width_kv)
     query_heads, kv_heads = (
         lax.all_to_all(query, "head", split_axis=3, concat_axis=2, tiled=True),
-        lax.all_to_all(stacked, "head", split_axis=3, concat_axis=2, tiled=True),
+        exchange_in_pairs(stacked, "head", 3, 2),
     )
     kv_local = kv_heads.shape[3] // HEAD_WIDTH
     heads_per_group = QUERY_HEADS // KEY_VALUE_HEADS

time: 156 us -> 150 us (0.962)
  blocking collectives: 27 us -> 17 us
  waiting for transfers between devices: 17.2 us -> 21.1 us
  local copies, waits for them, and re-layouts: 46 us -> 42.7 us
  starting transfers between devices: 3.52 us -> 6.7 us
    all_to_all x1 -> x0, blocking collectives: 10.1 us -> none  [local(): lax.all_to_all(stacked, 'head', split_axis=3, concat_axis=2, tiled=True)]
    ppermute x0 -> x3, waiting for transfers between devices: none -> 3.99 us  [exchange_in_pairs(): part = lax.ppermute(part, axis, [(d, d ^ mask) for d in range(ways)])]
    ppermute x0 -> x3, starting transfers between devices: none -> 3.18 us  [exchange_in_pairs(): part = lax.ppermute(part, axis, [(d, d ^ mask) for d in range(ways)])]
    unnamed x10 -> x7, local copies, waits for them, and re-layouts: 23.3 us -> 20.3 us
  transfers between devices with their start and end apart: 2 -> 5, of which waited for: 2 -> 4; matrix products, arithmetic and copies ran while one was open for 19% -> 20% of each run, Pallas kernels for 0% -> 0%
where the time goes in v1:
time: 150 us; the launch traced here: 149 us
  local copies, waits for them, and re-layouts  42.7 us (28%)
  matrix products  34.3 us (23%)
  waiting for transfers between devices  21.1 us (14%)
  blocking collectives  17 us (11%)
  between operations  13.5 us (9%)
  other arithmetic  13.2 us (9%)
  starting transfers between devices  6.7 us (4%)
    unnamed x7, local copies, waits for them, and re-layouts  20.3 us
    dot_general x2, matrix products, advance(): jnp.einsum('gjrk,kgd->rgjd', probs.astype(jnp.bfloat16), value_rows, pref...  20 us
    all_to_all x1, blocking collectives, local(): lax.all_to_all(result, 'head', split_axis=2, concat_axis=3, tiled=True)  17 us
    dot_general x2, matrix products, advance(): jnp.einsum('rgjd,kgd->gjrk', query_rows, key_row_block, preferred_element...  14.3 us
    all_to_all x1, waiting for transfers between devices, local(): lax.all_to_all(query, 'head', split_axis=3, concat_axis=2, tiled=True)  13.4 us
    all_to_all x1, local copies, waits for them, and re-layouts, local(): lax.all_to_all(query, 'head', split_axis=3, concat_axis=2, tiled=True)  8.97 us
    reduce_sum x2, other arithmetic, advance(): totals = totals * rescale + jnp.sum(probs, axis=-1)  7.97 us
    ppermute x3, waiting for transfers between devices, exchange_in_pairs(): part = lax.ppermute(part, axis, [(d, d ^ mask) for d in range(ways)])  3.99 us
  transfers between devices with their start and end apart: 5, of which 4 were waited for; matrix products, arithmetic and copies ran while one was open for 20% of the time, Pallas kernels for 0%

profile of v1, /device:TPU:0, one launch (start us, length us, event | category | flops | bytes accessed | tf_op | source)
XLA Modules:
  0.0 148.7 jit_solution(17407078603949474080)
XLA Ops:
  6.5 0.0 all-gather.2.cloned.1.call-start
  6.6 1.0 constant_dynamic-slice_fusion.1
  7.5 0.6 collective-permute-start
  8.1 2.6 %collective-permute-start.1 = (bf16[1,4,32,256]{3,2,1,0:T(8,128)(2,1)S(1)}, bf16[1,4,32,256]{3,2,1,0:T(8,128)(2,1)S(1)}, u32[]{:S(2)}, u32[]{:S(2)}) collective-permute-start(bf16[1,4,32,256]{3,2,1,0:T(8,128)(2,1)S(1)} %get-tuple-element.208), channel_id=1, source_target_pairs={{0,2},{1,3},{2,0},{3,1},{4,6},{5,7},{6,4},{7,5},{8,10},{9,11},{10,... | collective-permute-start | bytes 196616 | tf_op jit(solution)/shard_map/ppermute | solution.py:23
  10.7 0.0 collective-permute-start.2
  10.7 0.0 collective-permute-done
  10.7 2.6 %collective-permute-done.1 = bf16[1,4,32,256]{3,2,1,0:T(8,128)(2,1)S(1)} collective-permute-done((bf16[1,4,32,256]{3,2,1,0:T(8,128)(2,1)S(1)}, bf16[1,4,32,256]{3,2,1,0:T(8,128)(2,1)S(1)}, u32[]{:S(2)}, u32[]{:S(2)}) %collective-permute-start.1) | collective-permute-done | bytes 65568 | tf_op jit(solution)/shard_map/ppermute | solution.py:23
  13.4 1.4 collective-permute-done.2
  14.7 0.0 copy-start.1
  14.8 0.7 copy-done.1
  15.4 0.0 all-gather.2.cloned.1.call-update
  15.5 9.2 %copy.43 = bf16[1,2,32,8192]{2,1,0,3:T(2,128)(2,1)} copy(bf16[1,2,32,8192]{3,2,1,0:T(8,128)(2,1)} %param.5) | data formatting | bytes 2097152 | tf_op args[0]
  24.6 6.5 %reshape.200 = bf16[4,2,65536]{2,1,0:T(2,128)(2,1)} reshape(bf16[8192,1,2,32]{3,2,1,0:T(2,128)(2,1)} %bitcast.81) | data formatting | bytes 2097152
  31.1 3.5 %all-to-all-start = ((bf16[4,2,65536]{2,1,0:T(2,128)(2,1)}), bf16[4,2,65536]{2,1,0:T(2,128)(2,1)S(1)}, u32[]{:S(2)}, u32[]{:S(2)}) async-start(bf16[4,2,65536]{2,1,0:T(2,128)(2,1)} %reshape.200), calls=%async_computation | async-start | bytes 2097152 | tf_op jit(solution)/shard_map/all_to_all | solution.py:39
  34.7 0.8 reduce-window.7
  35.5 0.1 convert_reduce_fusion.1
  35.6 13.4 %all-to-all-done = bf16[4,2,65536]{2,1,0:T(2,128)(2,1)S(1)} async-done(((bf16[4,2,65536]{2,1,0:T(2,128)(2,1)}), bf16[4,2,65536]{2,1,0:T(2,128)(2,1)S(1)}, u32[]{:S(2)}, u32[]{:S(2)}) %all-to-all-start) | async-done | bytes 1048608 | tf_op jit(solution)/shard_map/all_to_all | solution.py:39
  49.0 3.5 %reshape.201 = bf16[8192,1,2,32]{3,2,1,0:T(2,128)(2,1)} reshape(bf16[4,2,65536]{2,1,0:T(2,128)(2,1)S(1)} %all-to-all-done) | data formatting | bytes 2097152
  52.5 9.0 %copy.44 = bf16[1,2,32,4,2048]{4,2,3,1,0:T(8,128)(2,1)S(1)} copy(bf16[1,2,32,4,2048]{2,1,4,3,0:T(2,128)(2,1)} %bitcast.80) | data formatting | bytes 2097152 | tf_op jit(solution)/shard_map/all_to_all | solution.py:39
  61.5 0.2 copy.63
  61.8 0.3 copy.46
  62.0 3.6 %all-gather.2.cloned.1.call-done = bf16[8,2,2,128,256]{4,3,2,1,0:T(8,128)(2,1)} async-done(((bf16[1,2,2,128,256]{4,3,2,1,0:T(8,128)(2,1)}), bf16[8,2,2,128,256]{4,3,2,1,0:T(8,128)(2,1)}) %all-gather.2.cloned.1.call-update) | async-done | bytes 2097168 | tf_op jit(solution)/shard_map/all_gather | solution.py:59
  65.7 52.6 %while.16 = (s32[]{:T(128)}, f32[2,8,256]{2,1,0:T(8,128)S(1)}, f32[2,8,256]{2,1,0:T(8,128)S(1)}, f32[256,2,8,128]{0,3,2,1:T(8,128)}, s32[256]{0:T(256)S(1)}, /*i...) while((s32[]{:T(128)}, f32[2,8,256]{2,1,0:T(8,128)S(1)}, ...), condition=%wide.region_6.7_spmd.clone.clone, body=%wide.region_2.6_spmd.clone.clone.sunk | while | flops 2204406784 | bytes 131365624 | solution.py:100
  65.7 0.6 dynamic_slice.37
  66.3 0.6 subtract_multiply_fusion.2
  66.9 0.1 iota_add_fusion.7
  67.0 0.1 iota_add_fusion.8
  67.1 0.1 convert_reduce_fusion.3
  67.2 0.3 compare_and_fusion.2
  67.5 1.3 copy_bitcast_fusion.2
  68.8 0.1 fusion.32
  68.9 0.1 squeeze.23
  69.0 7.2 %fusion.33 = (f32[2,8,256]{2,1,0:T(8,128)S(1)}, f32[2,1024,256,8]{2,1,3,0:T(8,128)}) fusion(pred[256,1024]{0,1:T(8,128)(4,1)S(1)} %compare_and_fusion.2, bf16[256,2,8,128]{3,0,2,1:T(8,128)(2,1)S(1)} %get-tuple-element.323, bf16[1024,2,128,1]{2,1,0,3:T(2,128)(2,1)S(1)} %bitcast.79), kind=kOutput, calls=%fused_computation.3.clone.1 | convolution fusion | flops 1086320640 | bytes 18628608 | tf_op jit(solution)/shard_map/while/body/eval_jaxpr/rgjd,kgd->gjrk/dot_general | solution.py:80
  76.2 0.1 reshape.203
  76.3 0.0 copy-start
  76.4 9.7 %bitcast_add_fusion.2 = f32[256,2,8,128]{0,3,2,1:T(8,128)} fusion(f32[256,2,8,128]{0,3,2,1:T(8,128)} %get-tuple-element.305, f32[2,1024,256,8]{2,1,3,0:T(8,128)} %get-tuple-element.287, f32[2,8,256]{2,1,0:T(8,128)S(1)} %get-tuple-element.315, pred[256,1024]{0,1:T(8,128)(4,1)S(1)} %compare_and_fusion.2, f32[256,2,8]{0,2,1:T(8,128)S(1)} %get-tuple-element.288, ...), kind=kOutput, calls=%fused_computation.8.clone.1 | convolution fusion | flops 1096286208 | bytes 21790720 | tf_op jit(solution)/shard_map/while/body/eval_jaxpr/gjrk,kgd->rgjd/dot_general | solution.py:90
  86.1 1.6 %copy-done = f32[2,1024,256,8]{2,1,3,0:T(8,128)S(1)} copy-done((f32[2,1024,256,8]{2,1,3,0:T(8,128)S(1)}, f32[2,1024,256,8]{2,1,3,0:T(8,128)}, u32[]{:S(2)}) %copy-start) | copy-done | bytes 16777240 | tf_op jit(solution)/shard_map/while
  87.6 4.0 %fusion.35 = f32[2,8,256]{2,1,0:T(8,128)S(1)} fusion(f32[2,1024,256,8]{2,1,3,0:T(8,128)S(1)} %copy-done, f32[2,8,256]{2,1,0:T(8,128)S(1)} %get-tuple-element.315, pred[256,1024]{0,1:T(8,128)(4,1)S(1)} %compare_and_fusion.2), kind=kLoop, calls=%fused_computation.5.clone.1 | loop fusion | flops 20967424 | bytes 17072128 | tf_op jit(solution)/shard_map/while/body/eval_jaxpr/reduce_sum | solution.py:89
  91.7 0.6 dynamic_slice.37
  92.3 0.6 subtract_multiply_fusion.2
  92.9 0.1 iota_add_fusion.7
  93.0 0.1 iota_add_fusion.8
  93.1 0.1 convert_reduce_fusion.3
  93.2 0.3 compare_and_fusion.2
  93.5 1.3 copy_bitcast_fusion.2
  94.8 0.1 fusion.32
  94.9 0.1 squeeze.23
  95.1 7.2 %fusion.33 = (f32[2,8,256]{2,1,0:T(8,128)S(1)}, f32[2,1024,256,8]{2,1,3,0:T(8,128)}) fusion(pred[256,1024]{0,1:T(8,128)(4,1)S(1)} %compare_and_fusion.2, bf16[256,2,8,128]{3,0,2,1:T(8,128)(2,1)S(1)} %get-tuple-element.323, bf16[1024,2,128,1]{2,1,0,3:T(2,128)(2,1)S(1)} %bitcast.79), kind=kOutput, calls=%fused_computation.3.clone.1 | convolution fusion | flops 1086320640 | bytes 18628608 | tf_op jit(solution)/shard_map/while/body/eval_jaxpr/rgjd,kgd->gjrk/dot_general | solution.py:80
  102.2 0.1 reshape.203
  102.4 0.0 copy-start
  102.4 10.3 %bitcast_add_fusion.2 = f32[256,2,8,128]{0,3,2,1:T(8,128)} fusion(f32[256,2,8,128]{0,3,2,1:T(8,128)} %get-tuple-element.305, f32[2,1024,256,8]{2,1,3,0:T(8,128)} %get-tuple-element.287, f32[2,8,256]{2,1,0:T(8,128)S(1)} %get-tuple-element.315, pred[256,1024]{0,1:T(8,128)(4,1)S(1)} %compare_and_fusion.2, f32[256,2,8]{0,2,1:T(8,128)S(1)} %get-tuple-element.288, ...), kind=kOutput, calls=%fused_computation.8.clone.1 | convolution fusion | flops 1096286208 | bytes 21790720 | tf_op jit(solution)/shard_map/while/body/eval_jaxpr/gjrk,kgd->rgjd/dot_general | solution.py:90
  112.7 1.6 %copy-done = f32[2,1024,256,8]{2,1,3,0:T(8,128)S(1)} copy-done((f32[2,1024,256,8]{2,1,3,0:T(8,128)S(1)}, f32[2,1024,256,8]{2,1,3,0:T(8,128)}, u32[]{:S(2)}) %copy-start) | copy-done | bytes 16777240 | tf_op jit(solution)/shard_map/while
  114.2 4.0 %fusion.35 = f32[2,8,256]{2,1,0:T(8,128)S(1)} fusion(f32[2,1024,256,8]{2,1,3,0:T(8,128)S(1)} %copy-done, f32[2,8,256]{2,1,0:T(8,128)S(1)} %get-tuple-element.315, pred[256,1024]{0,1:T(8,128)(4,1)S(1)} %compare_and_fusion.2), kind=kLoop, calls=%fused_computation.5.clone.1 | loop fusion | flops 20967424 | bytes 17072128 | tf_op jit(solution)/shard_map/while/body/eval_jaxpr/reduce_sum | solution.py:89
  118.3 1.8 %divide_convert_fusion = bf16[256,2,8,128]{0,3,2,1:T(8,128)(2,1)S(1)} fusion(f32[256,2,8,128]{0,3,2,1:T(8,128)} %get-tuple-element.66, f32[256,2,8]{0,2,1:T(8,128)S(1)} %bitcast.90), kind=kLoop, calls=%fused_computation.31 | loop fusion | flops 1048576 | bytes 3162112 | tf_op jit(solution)/shard_map/convert_element_type | solution.py:102
  120.1 0.3 reshape.198
  120.4 3.1 %copy.48 = bf16[1,2,128,2048]{3,1,0,2:T(2,128)(2,1)S(1)} copy(bf16[1,2,128,2048]{2,1,3,0:T(2,128)(2,1)S(1)} %reshape.198) | data formatting | bytes 2097152 | tf_op jit(solution)/shard_map/reshape | solution.py:103
  123.4 17.0 %all_to_all.33 = bf16[1,2,128,2048]{3,1,0,2:T(2,128)(2,1)S(1)} all-to-all(bf16[1,2,128,2048]{3,1,0,2:T(2,128)(2,1)S(1)} %copy.48), channel_id=1, replica_groups=mesh['ctx'=8,'head'=4] {'head'}, dimensions={2} | all-to-all | bytes 2097152 | tf_op jit(solution)/shard_map/all_to_all | solution.py:104
  140.4 0.3 copy.49
  140.8 1.0 copy.62
  (19 shorter events, 0.1 us)
Async XLA Ops:
  6.5 59.1 %all-gather.2.cloned.1.call-start = ((), (), s32[]{:S(2)}) async-start(), calls=%async_computation.2 | async-start | bytes 2359296 | tf_op jit(solution)/shard_map/all_gather | solution.py:59
  7.5 3.2 %collective-permute-start = (bf16[1,4,32,256]{3,2,1,0:T(8,128)(2,1)S(1)}, bf16[1,4,32,256]{3,2,1,0:T(8,128)(2,1)S(1)}, u32[]{:S(2)}, u32[]{:S(2)}) collective-permute-start(bf16[1,4,32,256]{3,2,1,0:T(8,128)(2,1)S(1)} %get-tuple-element.209), channel_id=1, source_target_pairs={{0,1},{1,0},{2,3},{3,2},{4,5},{5,4},{6,7},{7,6},{8,9},{9,8},{10,11... | collective-permute-start | bytes 196616 | tf_op jit(solution)/shard_map/ppermute | solution.py:23
  8.1 5.3 %collective-permute-start.1 = (bf16[1,4,32,256]{3,2,1,0:T(8,128)(2,1)S(1)}, bf16[1,4,32,256]{3,2,1,0:T(8,128)(2,1)S(1)}, u32[]{:S(2)}, u32[]{:S(2)}) collective-permute-start(bf16[1,4,32,256]{3,2,1,0:T(8,128)(2,1)S(1)} %get-tuple-element.208), channel_id=1, source_target_pairs={{0,2},{1,3},{2,0},{3,1},{4,6},{5,7},{6,4},{7,5},{8,10},{9,11},{10,... | collective-permute-start | bytes 196616 | tf_op jit(solution)/shard_map/ppermute | solution.py:23
  10.7 4.1 %collective-permute-start.2 = (bf16[1,4,32,256]{3,2,1,0:T(8,128)(2,1)S(1)}, bf16[1,4,32,256]{3,2,1,0:T(8,128)(2,1)S(1)}, u32[]{:S(2)}, u32[]{:S(2)}) collective-permute-start(bf16[1,4,32,256]{3,2,1,0:T(8,128)(2,1)S(1)} %get-tuple-element.207), channel_id=1, source_target_pairs={{0,3},{1,2},{2,1},{3,0},{4,7},{5,6},{6,5},{7,4},{8,11},{9,10},{10,... | collective-permute-start | bytes 196616 | tf_op jit(solution)/shard_map/ppermute | solution.py:23
  14.7 0.7 copy-start.1
  31.1 17.9 %all-to-all-start = ((bf16[4,2,65536]{2,1,0:T(2,128)(2,1)}), bf16[4,2,65536]{2,1,0:T(2,128)(2,1)S(1)}, u32[]{:S(2)}, u32[]{:S(2)}) async-start(bf16[4,2,65536]{2,1,0:T(2,128)(2,1)} %reshape.200), calls=%async_computation | async-start | bytes 2097152 | tf_op jit(solution)/shard_map/all_to_all | solution.py:39
  76.3 11.3 %copy-start = (f32[2,1024,256,8]{2,1,3,0:T(8,128)S(1)}, f32[2,1024,256,8]{2,1,3,0:T(8,128)}, u32[]{:S(2)}) copy-start(f32[2,1024,256,8]{2,1,3,0:T(8,128)} %get-tuple-element.287) | copy-start | bytes 50331652 | tf_op jit(solution)/shard_map/while
  102.4 11.9 %copy-start = (f32[2,1024,256,8]{2,1,3,0:T(8,128)S(1)}, f32[2,1024,256,8]{2,1,3,0:T(8,128)}, u32[]{:S(2)}) copy-start(f32[2,1024,256,8]{2,1,3,0:T(8,128)} %get-tuple-element.287) | copy-start | bytes 50331652 | tf_op jit(solution)/shard_map/while
Sparse Core Ops, SparseCore 0:
  15.6 50.0 all-gather.1
